TPU v7x, 32 devices: a whole 2x2x4 slice. The times are simulated.
32 devices in a mesh: seq: 16 (over z, y, x), head: 2 (over core).
Axes of the slice: x: 2, y: 2, z: 4, core: 2. Of those that a mesh axis runs over, the one named last changes fastest.
Arguments:
- queries: bfloat16 [8192, 2048], P('seq', 'head'), may hold values from -37.123106012293746 to 37.123106012293746
- keys: bfloat16 [8192, 2048], P('seq', 'head'), may hold values from -6 to 6
- values: bfloat16 [8192, 2048], P('seq', 'head'), may hold values from -24 to 24
- rand_blocks: int32 [128, 16], P('seq', 'head'), may hold values from 0 to 127, as said below
- global_blocks: int32 [2], replicated, may hold values from 0 to 127
- out_weight: bfloat16 [2048, 4096], P(('head', 'seq')), may hold values from -0.125 to 0.125
Outputs:
- layer_out: bfloat16 [8192, 4096], P(('seq', 'head'))
Inputs may be any that keep to these rules, and one draw needn't show every extreme that they name: `rand_blocks`: of the 8 x 8 entries of one device, at most 8 name blocks of one and the same index of seq (block id // 8), and some index of seq is named exactly 8 times by them.
All inputs are finite; a program needn't handle non-finite values.
Results may differ from a plain program's by a relative error of at most 0.013.
Values may be sent and summed in bfloat16 or wider, within the bound.
A program may use at most 128 MiB of HBM per device.

v0:
```python
import jax
import jax.numpy as jnp
from jax import lax
from jax.sharding import PartitionSpec as P


def padded_2(block, sides, width):
    for axis, dim in sides:
        count = lax.axis_size(axis)
        forward = [(i, i + 1) for i in range(count - 1)]
        forward.append((count - 1, 0))
        backward = [(target, source) for source, target in forward]
        low = lax.ppermute(
            lax.slice_in_dim(block, block.shape[dim] - width, None, axis=dim), axis, forward
        )
        high = lax.ppermute(lax.slice_in_dim(block, 0, width, axis=dim), axis, backward)
        block = jnp.concatenate([low, block, high], axis=dim)
    return block


def broadcast(value, axis, source):
    kept = jnp.where(lax.axis_index(axis) == source, value, 0).astype(value.dtype)
    return lax.psum(kept, axis)


def ranked(owners):
    count = owners.shape[0]
    order = jnp.arange(count, dtype=jnp.int32)
    earlier = (owners[:, None] == owners[None, :]) & (order[None, :] < order[:, None])
    return jnp.sum(earlier.astype(jnp.int32), axis=1)


def body(queries, keys, values, rand_blocks, global_blocks, out_weight):
    f32 = jnp.float32
    seq_count = lax.axis_size("seq")
    block_count, head_count = rand_blocks.shape
    block_len = queries.shape[0] // block_count
    head_dim = queries.shape[1] // head_count
    entries = block_count * head_count
    slot_cap = max(2, (2 * entries + seq_count - 1) // seq_count)
    global_count = global_blocks.shape[0]
    paired = jnp.stack([keys, values], axis=1)
    padded = padded_2(paired, (("seq", 0),), block_len)
    framed = padded.reshape(block_count + 2, block_len, 2, head_count, head_dim)
    window = jnp.concatenate([framed[:-2], framed[1:-1], framed[2:]], axis=1)
    holders = global_blocks // block_count
    offsets = global_blocks % block_count * block_len
    gathered = []
    for member in range(global_count):
        piece = lax.dynamic_slice_in_dim(paired, offsets[member], block_len, 0)
        gathered.append(broadcast(piece, "seq", holders[member]))
    shared = jnp.concatenate(gathered, axis=0)
    shared = shared.reshape(global_count * block_len, 2, head_count, head_dim)
    flat_blocks = rand_blocks.reshape(entries)
    owners = flat_blocks // block_count
    head_iota = jnp.arange(entries, dtype=jnp.int32) % head_count
    codes = flat_blocks % block_count * head_count + head_iota + 1
    slots = owners * slot_cap + ranked(owners)
    hits = slots[:, None] == jnp.arange(seq_count * slot_cap, dtype=jnp.int32)[None, :]
    outgoing = jnp.sum(jnp.where(hits, codes[:, None], 0), axis=0).reshape(seq_count, slot_cap)
    incoming = lax.all_to_all(outgoing, "seq", split_axis=0, concat_axis=0, tiled=True)
    wanted = incoming.reshape(seq_count * slot_cap)
    valid = wanted > 0
    code_less = jnp.maximum(wanted - 1, 0)
    blocked = paired.reshape(block_count, block_len, 2, head_count, head_dim)
    picked = blocked[code_less // head_count, :, :, code_less % head_count, :]
    picked = jnp.where(valid[:, None, None, None], picked, jnp.zeros_like(picked))
    arrived = lax.all_to_all(
        picked.reshape(seq_count, slot_cap, block_len, 2, head_dim),
        "seq",
        split_axis=0,
        concat_axis=0,
        tiled=True,
    )
    chosen = arrived.reshape(seq_count * slot_cap, block_len, 2, head_dim)[slots]
    chosen = chosen.reshape(block_count, head_count, block_len, 2, head_dim)
    query_blocks = queries.reshape(block_count, block_len, head_count, head_dim)
    s_window = jnp.einsum(
        "qbhd,qkhd->qhbk", query_blocks, window[:, :, 0], preferred_element_type=f32
    )
    s_global = jnp.einsum("qbhd,khd->qhbk", query_blocks, shared[:, 0], preferred_element_type=f32)
    s_random = jnp.einsum(
        "qbhd,qhkd->qhbk", query_blocks, chosen[:, :, :, 0], preferred_element_type=f32
    )
    scores = jnp.concatenate([s_window, s_global, s_random], axis=-1) * head_dim ** (-0.5)
    top = jnp.max(scores, axis=-1, keepdims=True)
    expo = jnp.exp(scores - top)
    weights = (expo / jnp.sum(expo, axis=-1, keepdims=True)).astype(jnp.bfloat16)
    wlen = window.shape[1]
    glen = shared.shape[0]
    context = jnp.einsum(
        "qhbk,qkhd->qbhd", weights[..., :wlen], window[:, :, 1], preferred_element_type=f32
    )
    context = context + jnp.einsum(
        "qhbk,khd->qbhd", weights[..., wlen : wlen + glen], shared[:, 1], preferred_element_type=f32
    )
    context = context + jnp.einsum(
        "qhbk,qhkd->qbhd",
        weights[..., wlen + glen :],
        chosen[:, :, :, 1],
        preferred_element_type=f32,
    )
    attended = context.reshape(block_count * block_len, head_count * head_dim).astype(jnp.bfloat16)
    group_rows = lax.all_gather(out_weight, "seq", axis=0, tiled=True)
    partial_value = jnp.dot(attended, group_rows, preferred_element_type=f32)
    summed = lax.psum_scatter(
        partial_value.astype(jnp.bfloat16), "head", scatter_dimension=0, tiled=True
    )
    return summed


def solution(mesh):
    placed = (
        P("seq", "head"),
        P("seq", "head"),
        P("seq", "head"),
        P("seq", "head"),
        P(),
        P(("head", "seq"), None),
    )
    return jax.shard_map(
        body, mesh=mesh, in_specs=placed, out_specs=P(("seq", "head"), None), check_vma=False
    )
```

profile of v0, /device:TPU:0, one launch (start us, length us, event | category | flops | bytes accessed | tf_op | source)
XLA Modules:
  0.0 325.4 jit_solution(5017997300551547966)
XLA Ops:
  6.5 0.7 and_select_fusion.7
  7.2 0.6 fusion.40
  11.5 1.5 copy.57
  13.0 1.9 copy.58
  14.9 0.0 copy-start.8
  14.9 0.0 copy-start.5
  16.2 2.1 fusion.20
  18.2 0.0 all-reduce.3.cloned.1.call-update
  18.3 0.0 all-gather.2.cloned.1.call-start
  18.3 0.7 all-gather.2.cloned.1.call-update
  19.0 0.1 reshape.309
  19.1 0.2 convert_reduce_fusion
  19.3 0.1 select_reduce_fusion
  19.4 0.7 all_to_all.9
  20.1 8.3 %all-to-all-start = ((s32[16,1,8]{2,1,0:T(1,128)}), s32[16,1,8]{2,1,0:T(1,128)S(1)}, u32[]{:S(2)}, u32[]{:S(2)}) async-start(s32[16,1,8]{2,1,0:T(1,128)} %bitcast.13), calls=%async_computation | async-start | bytes 16384 | tf_op jit(solution)/shard_map/all_to_all | solution.py:61
  28.5 0.3 copy.85
  28.8 1.5 copy.86
  30.3 0.3 copy_dynamic-update-slice_fusion.1
  30.5 0.4 copy_dynamic-update-slice_fusion
  30.9 4.8 %all-to-all-done = s32[16,1,8]{2,1,0:T(1,128)S(1)} async-done(((s32[16,1,8]{2,1,0:T(1,128)}), s32[16,1,8]{2,1,0:T(1,128)S(1)}, u32[]{:S(2)}, u32[]{:S(2)}) %all-to-all-start) | async-done | bytes 544 | tf_op jit(solution)/shard_map/all_to_all | solution.py:61
  35.8 0.1 copy.69
  35.8 0.1 copy.74
  35.9 0.1 div.60
  36.0 0.1 copy.73
  36.1 0.1 rem.106
  36.2 0.1 copy.72
  36.3 0.1 ne.157
  36.4 0.1 copy.70
  36.5 3.1 gather_fusion
  39.6 4.6 %broadcast_select_fusion = bf16[16,8,64,2,128]{4,2,3,1,0:T(8,128)(2,1)} fusion(bf16[16,8,64,2,128]{4,2,3,1,0:T(8,128)(2,1)} %bitcast.92, pred[16,8]{1,0:T(8,128)(4,1)S(1)} %copy.70), kind=kLoop, calls=%fused_computation.8 | loop fusion | flops 2097152 | bytes 8388736 | tf_op jit(solution)/shard_map/jit(_where)/select_n | solution.py:67
  44.1 4.5 %all-to-all-start.1 = ((bf16[16,8,64,2,128]{4,2,3,1,0:T(8,128)(2,1)}), bf16[16,8,64,2,128]{4,2,3,1,0:T(8,128)(2,1)}, u32[]{:S(2)}, u32[]{:S(2)}) async-start(bf16[16,8,64,2,128]{4,2,3,1,0:T(8,128)(2,1)} %broadcast_select_fusion), calls=%async_computation.1 | async-start | bytes 8388608 | tf_op jit(solution)/shard_map/all_to_all | solution.py:68
  48.7 0.0 reduce-scatter.2.cloned.1.call-start
  48.7 1.8 collective-permute-start
  50.5 3.9 %collective-permute-start.1 = (bf16[64,2,1024]{0,2,1:T(8,128)(2,1)}, bf16[64,2,1024]{0,2,1:T(8,128)(2,1)}, u32[]{:S(2)}, u32[]{:S(2)}) collective-permute-start(bf16[64,2,1024]{0,2,1:T(8,128)(2,1)} %get-tuple-element.10), channel_id=1, source_target_pairs={{2,0},{4,2},{6,4},{8,6},{10,8},{12,10},{14,12},{16,14},{18,16},{20... | collective-permute-start | bytes 786440 | tf_op jit(solution)/shard_map/ppermute | solution.py:16
  54.5 0.1 reshape.311
  54.6 1.5 copy.87
  56.1 80.8 %collective-permute-done = bf16[64,2,1024]{0,2,1:T(8,128)(2,1)} collective-permute-done((bf16[64,2,1024]{0,2,1:T(8,128)(2,1)}, bf16[64,2,1024]{0,2,1:T(8,128)(2,1)}, u32[]{:S(2)}, u32[]{:S(2)}) %collective-permute-start) | collective-permute-done | bytes 262176 | tf_op jit(solution)/shard_map/ppermute | solution.py:13
  136.9 6.5 %pad_maximum_fusion.3 = (bf16[512,2,1024]{0,2,1:T(8,128)(2,1)}, bf16[512,2,1024]{0,2,1:T(8,128)(2,1)}) fusion(bf16[64,2,1024]{0,2,1:T(8,128)(2,1)} %collective-permute-done, bf16[512,1,1024]{0,2,1:T(8,128)(2,1)} %bitcast.99, bf16[512,1,1024]{0,2,1:T(8,128)(2,1)} %bitcast.97, bf16[64,2,1024]{0,2,1:T(8,128)(2,1)} %collective-permute-done.1), kind=kLoop, calls=%fused_computation.26 | loop fusion | flops 12582912 | bytes 6815744 | tf_op jit(solution)/shard_map/concatenate | solution.py:17
  143.4 6.3 %reshape.329 = bf16[8,64,2,8,128]{1,0,4,3,2:T(8,128)(2,1)} reshape(bf16[512,2,1024]{0,2,1:T(8,128)(2,1)} %get-tuple-element.7) | data formatting | bytes 4194304 | tf_op jit(solution)/shard_map/slice | solution.py:45
  149.6 5.5 %copy.63 = bf16[8,64,2,8,128]{4,1,3,0,2:T(8,128)(2,1)} copy(bf16[8,64,2,8,128]{1,0,4,3,2:T(8,128)(2,1)} %reshape.329) | data formatting | bytes 4194304 | tf_op jit(solution)/shard_map/slice | solution.py:45
  155.1 6.3 %reshape.330 = bf16[8,64,2,8,128]{1,0,4,3,2:T(8,128)(2,1)} reshape(bf16[512,2,1024]{0,2,1:T(8,128)(2,1)} %get-tuple-element.8) | data formatting | bytes 4194304 | tf_op jit(solution)/shard_map/slice | solution.py:45
  161.4 5.5 %copy.64 = bf16[8,64,2,8,128]{4,1,3,0,2:T(8,128)(2,1)} copy(bf16[8,64,2,8,128]{1,0,4,3,2:T(8,128)(2,1)} %reshape.330) | data formatting | bytes 4194304 | tf_op jit(solution)/shard_map/slice | solution.py:45
  166.9 3.1 pad_maximum_fusion
  170.1 2.7 copy-done
  172.8 4.2 %fusion.4 = f32[8,8,64,192]{3,2,1,0:T(8,128)} fusion(bf16[8,192,2,8,128]{4,1,3,0,2:T(8,128)(2,1)S(1)} %pad_maximum_fusion, bf16[8,64,8,128]{3,2,1,0:T(8,128)(2,1)S(1)} %bitcast.93), kind=kOutput, calls=%fused_computation.22 | convolution fusion | flops 201326592 | bytes 7340032 | tf_op jit(solution)/shard_map/qbhd,qkhd->qhbk/dot_general | solution.py:78
  176.9 7.7 %all-reduce.3.cloned.1.call-done = (bf16[64,2,1024]{0,2,1:T(8,128)(2,1)}, bf16[64,2,1024]{0,2,1:T(8,128)(2,1)}) async-done(((bf16[64,2,1024]{0,2,1:T(8,128)(2,1)}, bf16[64,2,1024]{0,2,1:T(8,128)(2,1)}), (bf16[64,2,1024]{0,2,1:T(8,128)(2,1)}, bf16[64,2,1024]{0,2,1:T(8,128)(2,1)})) %all-reduce.3.cloned.1.call-update) | async-done | bytes 524304 | tf_op jit(solution)/shard_map/psum | solution.py:23
  184.7 1.5 pad_maximum_fusion.5
  186.2 1.7 convolution_bitcast_fusion.1
  187.9 3.1 gather_fusion.1
  191.1 0.2 copy.75
  191.3 0.7 convolution_bitcast_fusion
  191.9 0.7 copy-done.4
  192.6 1.3 copy-done.1
  193.9 17.6 %fusion.42 = (f32[8,8,64]{2,1,0:T(8,128)S(1)}, f32[8,8,64,384]{3,2,1,0:T(8,128)S(1)}) fusion(f32[8,8,64,64]{3,2,1,0:T(8,128)S(1)} %convolution_bitcast_fusion, f32[8,8,64,128]{3,2,1,0:T(8,128)S(1)} %copy-done.4, f32[8,8,64,192]{3,2,1,0:T(8,128)S(1)} %copy-done.1), kind=kOutput, calls=%fused_computation.103 | output fusion | flops 7864703 | bytes 12599296 | tf_op jit(solution)/shard_map/sub | solution.py:87
  211.6 0.7 divide_convert_fusion
  212.3 0.3 copy-done.7
  212.6 0.5 fusion.13
  213.1 0.5 fusion.11
  213.6 1.4 fusion.6
  215.1 0.7 copy.78
  215.8 83.3 %all-gather.2.cloned.1.call-done = bf16[1024,4096]{1,0:T(8,128)(2,1)} async-done(((bf16[64,4096]{1,0:T(8,128)(2,1)}), bf16[1024,4096]{1,0:T(8,128)(2,1)}) %all-gather.2.cloned.1.call-update) | async-done | bytes 8388624 | tf_op jit(solution)/shard_map/all_gather | solution.py:104
  299.1 9.4 %convolution_convert_fusion = bf16[512,4096]{1,0:T(8,128)(2,1)} fusion(bf16[1024,4096]{1,0:T(8,128)(2,1)} %all-gather.2.cloned.1.call-done, bf16[64,8,8,128]{3,2,1,0:T(8,128)(2,1)S(1)} %bitcast.109), kind=kOutput, calls=%fused_computation.7 | convolution fusion | flops 4297064448 | bytes 13631488 | tf_op jit(solution)/shard_map/dot_general | solution.py:105
  308.5 0.0 reduce-scatter.2.cloned.1.call-update
  308.6 10.4 %reduce-scatter.2.cloned.1.call-done = bf16[256,4096]{1,0:T(8,128)(2,1)} async-done(((bf16[512,4096]{1,0:T(8,128)(2,1)}), bf16[256,4096]{1,0:T(8,128)(2,1)}) %reduce-scatter.2.cloned.1.call-update) | async-done | bytes 2097168 | tf_op jit(solution)/shard_map/reduce_scatter | solution.py:106
  (27 shorter events, 0.1 us)
Async XLA Ops:
  6.5 178.1 %all-reduce.3.cloned.1.call-start = ((), (), s32[]{:S(2)}) async-start(), calls=%async_computation.5 | async-start | bytes 2097152 | tf_op jit(solution)/shard_map/psum | solution.py:23
  13.0 5.3 %copy-start.2 = (bf16[512,1024]{0,1:T(8,128)(2,1)}, bf16[512,1024]{0,1:T(8,128)(2,1)S(1)}, u32[]{:S(2)}) copy-start(bf16[512,1024]{0,1:T(8,128)(2,1)S(1)} %copy.57) | copy-start | bytes 3145732
  14.9 13.9 %copy-start.3 = (bf16[512,1024]{0,1:T(8,128)(2,1)}, bf16[512,1024]{0,1:T(8,128)(2,1)S(1)}, u32[]{:S(2)}) copy-start(bf16[512,1024]{0,1:T(8,128)(2,1)S(1)} %copy.58) | copy-start | bytes 3145732
  14.9 4.1 %copy-start.8 = (s32[8,8]{1,0:T(8,128)S(1)}, s32[8,8]{1,0:T(8,128)}, u32[]{:S(2)}) copy-start(s32[8,8]{1,0:T(8,128)} %param.9) | copy-start | bytes 772
  14.9 13.6 %copy-start.5 = (bf16[512,1024]{1,0:T(8,128)(2,1)S(1)}, bf16[512,1024]{1,0:T(8,128)(2,1)}, u32[]{:S(2)}) copy-start(bf16[512,1024]{1,0:T(8,128)(2,1)} %param.7) | copy-start | bytes 3145732
  18.3 280.8 %all-gather.2.cloned.1.call-start = ((), (), s32[]{:S(2)}) async-start(), calls=%async_computation.3 | async-start | bytes 8912896 | tf_op jit(solution)/shard_map/all_gather | solution.py:104
  20.1 15.7 %all-to-all-start = ((s32[16,1,8]{2,1,0:T(1,128)}), s32[16,1,8]{2,1,0:T(1,128)S(1)}, u32[]{:S(2)}, u32[]{:S(2)}) async-start(s32[16,1,8]{2,1,0:T(1,128)} %bitcast.13), calls=%async_computation | async-start | bytes 16384 | tf_op jit(solution)/shard_map/all_to_all | solution.py:61
  44.1 143.8 %all-to-all-start.1 = ((bf16[16,8,64,2,128]{4,2,3,1,0:T(8,128)(2,1)}), bf16[16,8,64,2,128]{4,2,3,1,0:T(8,128)(2,1)}, u32[]{:S(2)}, u32[]{:S(2)}) async-start(bf16[16,8,64,2,128]{4,2,3,1,0:T(8,128)(2,1)} %broadcast_select_fusion), calls=%async_computation.1 | async-start | bytes 8388608 | tf_op jit(solution)/shard_map/all_to_all | solution.py:68
  48.7 270.2 %reduce-scatter.2.cloned.1.call-start = ((), (), s32[]{:S(2)}) async-start(), calls=%async_computation.4 | async-start | bytes 6291456 | tf_op jit(solution)/shard_map/reduce_scatter | solution.py:106
  48.7 88.1 %collective-permute-start = (bf16[64,2,1024]{0,2,1:T(8,128)(2,1)}, bf16[64,2,1024]{0,2,1:T(8,128)(2,1)}, u32[]{:S(2)}, u32[]{:S(2)}) collective-permute-start(bf16[64,2,1024]{0,2,1:T(8,128)(2,1)} %get-tuple-element.9), channel_id=1, source_target_pairs={{0,2},{2,4},{4,6},{6,8},{8,10},{10,12},{12,14},{14,16},{16,18},{18... | collective-permute-start | bytes 786440 | tf_op jit(solution)/shard_map/ppermute | solution.py:13
  50.5 86.4 %collective-permute-start.1 = (bf16[64,2,1024]{0,2,1:T(8,128)(2,1)}, bf16[64,2,1024]{0,2,1:T(8,128)(2,1)}, u32[]{:S(2)}, u32[]{:S(2)}) collective-permute-start(bf16[64,2,1024]{0,2,1:T(8,128)(2,1)} %get-tuple-element.10), channel_id=1, source_target_pairs={{2,0},{4,2},{6,4},{8,6},{10,8},{12,10},{14,12},{16,14},{18,16},{20... | collective-permute-start | bytes 786440 | tf_op jit(solution)/shard_map/ppermute | solution.py:16
  170.0 2.7 copy-start
  186.1 1.8 copy-start.6
  191.1 1.6 copy-start.4
  191.2 2.7 copy-start.1
  193.9 19.7 %slice-start = ((s8[6291456]{0:T(1024)(128)(4,1)}), s8[4194304]{0:T(1024)(128)(4,1)S(1)}, s32[]{:S(2)}) async-start(s8[6291456]{0:T(1024)(128)(4,1)} %bitcast.90), calls=%async_computation.6 | async-start | bytes 8388608
  211.5 1.0 copy-start.7
  211.6 2.1 slice-start.1
Sparse Core Ops, SparseCore 0:
  18.4 166.2 all-reduce.2
  187.4 111.6 all-gather.1
  308.7 10.1 reduce-scatter.1
where the time goes:
time: 327 us; the launch traced here: 325 us
  waiting for transfers between devices  188 us (57%)
  local copies, waits for them, and re-layouts  45.1 us (14%)
  other arithmetic  37.1 us (11%)
  starting transfers between devices  18.7 us (6%)
  matrix products  18.4 us (6%)
  between operations  18.4 us (6%)
    all_gather x1, waiting for transfers between devices, body(): group_rows = lax.all_gather(out_weight, 'seq', axis=0, tiled=True)  83.3 us
    ppermute x1, waiting for transfers between devices, padded_2(): lax.ppermute(lax.slice_in_dim(block, block.shape[dim] - width, None, axis...  80.8 us
    slice x4, local copies, waits for them, and re-layouts, body(): window = jnp.concatenate([framed[:-2], framed[1:-1], framed[2:]], axis=1)  23.5 us
    sub x1, other arithmetic, body(): expo = jnp.exp(scores - top)  17.6 us
    unnamed x28, local copies, waits for them, and re-layouts  11.9 us
    reduce_scatter x1, waiting for transfers between devices, body(): lax.psum_scatter(partial_value.astype(jnp.bfloat16), 'head', scatter_dime...  10.4 us
    dot_general x1, matrix products, body(): partial_value = jnp.dot(attended, group_rows, preferred_element_type=f32)  9.41 us
    all_to_all x1, starting transfers between devices, body(): lax.all_to_all(outgoing, 'seq', split_axis=0, concat_axis=0, tiled=True)  8.34 us
  transfers between devices with their start and end apart: 7, of which 5 were waited for; matrix products, arithmetic and copies ran while one was open for 24% of the time, Pallas kernels for 0%

commit v1 on v0

v1 whole, which is shorter than its diff:
```python
import functools

import jax
import jax.numpy as jnp
from jax import lax
from jax.experimental import pallas as pl
from jax.experimental.pallas import tpu as pltpu
from jax.sharding import PartitionSpec as P


def ranked(owners):
    count = owners.shape[0]
    order = jnp.arange(count, dtype=jnp.int32)
    earlier = (owners[:, None] == owners[None, :]) & (order[None, :] < order[:, None])
    return jnp.sum(earlier.astype(jnp.int32), axis=1)


def pack_kernel(cap, block_len, head_dim, head_count, codes_ref, k_ref, v_ref, g_ref, o_ref):
    dst = pl.program_id(0)
    for s in range(cap):
        code = codes_ref[dst * cap + s]
        row = pl.multiple_of(code // head_count * block_len, block_len)
        col = pl.multiple_of(code % head_count * head_dim, head_dim)
        rows = pl.ds(s * block_len, block_len)
        o_ref[0, rows, 0:head_dim] = k_ref[pl.ds(row, block_len), pl.ds(col, head_dim)]
        o_ref[0, rows, head_dim : 2 * head_dim] = v_ref[pl.ds(row, block_len), pl.ds(col, head_dim)]
    o_ref[0, cap * block_len :, :] = g_ref[0]


def pack(codes, keys, values, pieces, cap, block_len, head_dim, head_count):
    n, extra, width = pieces.shape
    rows = cap * block_len + extra
    whole = lambda d, c: (0, 0)
    return pl.pallas_call(
        functools.partial(pack_kernel, cap, block_len, head_dim, head_count),
        out_shape=jax.ShapeDtypeStruct((n, rows, width), keys.dtype),
        grid_spec=pltpu.PrefetchScalarGridSpec(
            num_scalar_prefetch=1,
            grid=(n,),
            in_specs=[
                pl.BlockSpec(keys.shape, whole),
                pl.BlockSpec(values.shape, whole),
                pl.BlockSpec((1, extra, width), lambda d, c: (d, 0, 0)),
            ],
            out_specs=pl.BlockSpec((1, rows, width), lambda d, c: (d, 0, 0)),
        ),
        cost_estimate=pl.CostEstimate(
            flops=0, transcendentals=0, bytes_accessed=2 * n * rows * width * 2
        ),
        name="pack",
    )(codes, keys, values, pieces)


def attend_kernel(
    blocks, block_len, head_dim, head_count, scale,
    own_ref, rank_ref, q_ref, k_ref, v_ref, low_ref, high_ref, kg_ref, vg_ref, arr_ref, o_ref,
):
    h = pl.program_id(0)
    kk = jnp.concatenate([low_ref[0], k_ref[...], high_ref[0]], axis=0)
    vv = jnp.concatenate([low_ref[1], v_ref[...], high_ref[1]], axis=0)
    kg, vg = kg_ref[...], vg_ref[...]
    for b in range(blocks):
        e = b * head_count + h
        owner = own_ref[e]
        rows = pl.ds(pl.multiple_of(rank_ref[e] * block_len, block_len), block_len)
        kr = arr_ref[owner, rows, 0:head_dim]
        vr = arr_ref[owner, rows, head_dim : 2 * head_dim]
        lo, hi = b * block_len, (b + 3) * block_len
        ks = jnp.concatenate([kk[lo:hi], kg, kr], axis=0)
        vs = jnp.concatenate([vv[lo:hi], vg, vr], axis=0)
        q = q_ref[lo : lo + block_len, :]
        s = lax.dot_general(
            q, ks, (((1,), (1,)), ((), ())), preferred_element_type=jnp.float32
        ) * scale
        top = jnp.max(s, axis=-1, keepdims=True)
        expo = jnp.exp(s - top)
        total = jnp.sum(expo, axis=-1, keepdims=True)
        w = (expo * (1.0 / total)).astype(jnp.bfloat16)
        o = jnp.dot(w, vs, preferred_element_type=jnp.float32)
        o_ref[lo : lo + block_len, :] = o.astype(o_ref.dtype)


def attend(owners, ranks, q, k, v, low, high, kg, vg, arrived, blocks, block_len, head_dim, head_count):
    tokens, width = q.shape
    col = lambda h, a, b: (0, h)
    edge = pl.BlockSpec((2, block_len, head_dim), lambda h, a, b: (0, 0, h))
    main = pl.BlockSpec((tokens, head_dim), col)
    glob = pl.BlockSpec((kg.shape[0], head_dim), col)
    return pl.pallas_call(
        functools.partial(
            attend_kernel, blocks, block_len, head_dim, head_count, head_dim ** (-0.5)
        ),
        out_shape=jax.ShapeDtypeStruct(q.shape, jnp.bfloat16),
        grid_spec=pltpu.PrefetchScalarGridSpec(
            num_scalar_prefetch=2,
            grid=(head_count,),
            in_specs=[
                main, main, main, edge, edge, glob, glob,
                pl.BlockSpec(arrived.shape, lambda h, a, b: (0, 0, 0)),
            ],
            out_specs=main,
        ),
        cost_estimate=pl.CostEstimate(
            flops=4 * tokens * 6 * block_len * width,
            transcendentals=tokens * 6 * block_len * head_count,
            bytes_accessed=2 * (4 * q.size + arrived.size),
        ),
        name="attend",
    )(owners, ranks, q, k, v, low, high, kg, vg, arrived)


def body(queries, keys, values, rand_blocks, global_blocks, out_weight):
    f32 = jnp.float32
    n = lax.axis_size("seq")
    block_count, head_count = rand_blocks.shape
    tokens, width = queries.shape
    block_len = tokens // block_count
    head_dim = width // head_count
    entries = block_count * head_count
    cap = max(2, (2 * entries + n - 1) // n)
    g = global_blocks.shape[0]
    wide = 2 * head_dim

    group_rows = lax.all_gather(out_weight, "seq", axis=0, tiled=True)

    flat_blocks = rand_blocks.reshape(entries)
    owners = flat_blocks // block_count
    head_iota = jnp.arange(entries, dtype=jnp.int32) % head_count
    codes = flat_blocks % block_count * head_count + head_iota
    ranks = ranked(owners)
    slots = owners * cap + ranks
    hits = slots[:, None] == jnp.arange(n * cap, dtype=jnp.int32)[None, :]
    outgoing = jnp.sum(jnp.where(hits, codes[:, None], 0), axis=0).reshape(n, cap)
    incoming = lax.all_to_all(outgoing, "seq", split_axis=0, concat_axis=0, tiled=True)
    wanted = incoming.reshape(n * cap)

    forward = [(i, (i + 1) % n) for i in range(n)]
    backward = [(t, s) for s, t in forward]
    low = lax.ppermute(jnp.stack([keys[-block_len:], values[-block_len:]]), "seq", forward)
    high = lax.ppermute(jnp.stack([keys[:block_len], values[:block_len]]), "seq", backward)

    holders = global_blocks // block_count
    offsets = global_blocks % block_count * block_len
    share = n // g
    thin = block_len * width // (share * head_dim)

    def cut(array, member):
        piece = lax.dynamic_slice_in_dim(array, offsets[member], block_len, 0)
        return piece.reshape(share, thin // 2, wide)

    pieces = jnp.concatenate(
        [jnp.concatenate([cut(keys, m), cut(values, m)], axis=1) for m in range(g)], axis=0
    )
    packed = pack(wanted, keys, values, pieces, cap, block_len, head_dim, head_count)
    arrived = lax.all_to_all(packed, "seq", split_axis=0, concat_axis=0, tiled=True)
    source = holders[lax.axis_index("seq") // share]
    mine = lax.dynamic_slice(arrived, (source, cap * block_len, 0), (1, thin, wide))
    shared = lax.all_gather(mine, "seq", axis=0, tiled=True)
    kg = shared[:, : thin // 2].reshape(g * block_len, width)
    vg = shared[:, thin // 2 :].reshape(g * block_len, width)

    attended = attend(
        owners, ranks, queries, keys, values, low, high, kg, vg, arrived,
        block_count, block_len, head_dim, head_count,
    )
    partial_value = jnp.dot(attended, group_rows, preferred_element_type=f32)
    return lax.psum_scatter(
        partial_value.astype(jnp.bfloat16), "head", scatter_dimension=0, tiled=True
    )


def solution(mesh):
    placed = (
        P("seq", "head"),
        P("seq", "head"),
        P("seq", "head"),
        P("seq", "head"),
        P(),
        P(("head", "seq"), None),
    )
    return jax.shard_map(
        body, mesh=mesh, in_specs=placed, out_specs=P(("seq", "head"), None), check_vma=False
    )
```

time: 327 us -> 321 us (0.982)
  blocking collectives: 0 us -> 65.1 us
  Pallas kernels: 0 us -> 37.5 us
  local copies, waits for them, and re-layouts: 45.1 us -> 9.77 us
  other arithmetic: 37.1 us -> 2.55 us
  waiting for transfers between devices: 188 us -> 154 us
  matrix products: 18.4 us -> 10.2 us
    all_to_all x1, waiting for transfers between devices: 0.01 us -> 145 us  [body(): lax.all_to_all(packed, 'seq', split_axis=0, concat_axis=0, tiled=True)]
    all_gather x1, waiting for transfers between devices: 83.3 us -> 0.01 us  [body(): group_rows = lax.all_gather(out_weight, 'seq', axis=0, tiled=True)]
    ppermute x2, waiting for transfers between devices: 80.8 us -> 0.01 us  [the longest x1 0.01 us: body(): lax.ppermute(jnp.stack([keys[:block_len], values[:block_len]]), 'seq', ba...]
    all_gather x0 -> x1, blocking collectives: none -> 65.1 us  [body(): shared = lax.all_gather(mine, 'seq', axis=0, tiled=True)]
    pallas_call x0 -> x2, Pallas kernels: none -> 37.5 us  [the longest x1 26.8 us: attend(): pl.pallas_call(functools.partial(attend_kernel, blocks, block_len, head_d...]
    slice x5 -> x2, local copies, waits for them, and re-layouts: 24.2 us -> 0.67 us  [the longest x1 0.64 us: cut(): piece = lax.dynamic_slice_in_dim(array, offsets[member], block_len, 0)]
    sub x1 -> x0, other arithmetic: 17.6 us -> none  [body(): expo = jnp.exp(scores - top)]
    unnamed x28 -> x8, local copies, waits for them, and re-layouts: 11.9 us -> 1.43 us
  transfers between devices with their start and end apart: 7 -> 6, of which waited for: 5 -> 2; matrix products, arithmetic and copies ran while one was open for 24% -> 3% of each run, Pallas kernels for 0% -> 12%
where the time goes in v1:
time: 321 us; the launch traced here: 319 us
  waiting for transfers between devices  154 us (48%)
  blocking collectives  65.1 us (20%)
  Pallas kernels  37.5 us (12%)
  starting transfers between devices  20.9 us (7%)
  between operations  19.3 us (6%)
  matrix products  10.2 us (3%)
  local copies, waits for them, and re-layouts  9.77 us (3%)
    all_to_all x1, waiting for transfers between devices, body(): lax.all_to_all(packed, 'seq', split_axis=0, concat_axis=0, tiled=True)  145 us
    all_gather x1, blocking collectives, body(): shared = lax.all_gather(mine, 'seq', axis=0, tiled=True)  65.1 us
    pallas_call x1, Pallas kernels, attend(): pl.pallas_call(functools.partial(attend_kernel, blocks, block_len, head_d...  26.8 us
    pallas_call x1, Pallas kernels, pack(): pl.pallas_call(functools.partial(pack_kernel, cap, block_len, head_dim, h...  10.7 us
    dot_general x1, matrix products, body(): partial_value = jnp.dot(attended, group_rows, preferred_element_type=f32)  10.2 us
    all_to_all x1, starting transfers between devices, body(): lax.all_to_all(outgoing, 'seq', split_axis=0, concat_axis=0, tiled=True)  8.34 us
    reduce_scatter x1, waiting for transfers between devices, body(): lax.psum_scatter(partial_value.astype(jnp.bfloat16), 'head', scatter_dime...  8.06 us
    all_to_all x1, starting transfers between devices, body(): lax.all_to_all(packed, 'seq', split_axis=0, concat_axis=0, tiled=True)  6.95 us
  transfers between devices with their start and end apart: 6, of which 2 were waited for; matrix products, arithmetic and copies ran while one was open for 3% of the time, Pallas kernels for 12%

profile of v1, /device:TPU:0, one launch (start us, length us, event | category | flops | bytes accessed | tf_op | source)
XLA Modules:
  0.0 319.3 jit_solution(2454071432655253138)
XLA Ops:
  6.5 0.0 all-gather.2.cloned.1.call-start
  6.5 0.7 all-gather.2.cloned.1.call-update
  7.3 0.8 reshape.130
  8.0 0.0 copy-start.2
  8.0 0.2 convert_reduce_fusion.rank_ref
  8.2 0.0 copy-start.3
  8.2 0.1 select_reduce_fusion
  8.3 0.7 all_to_all.9
  9.0 8.3 %all-to-all-start = ((s32[16,1,8]{2,1,0:T(1,128)}), s32[16,1,8]{2,1,0:T(1,128)S(1)}, u32[]{:S(2)}, u32[]{:S(2)}) async-start(s32[16,1,8]{2,1,0:T(1,128)} %bitcast.4), calls=%async_computation | async-start | bytes 16384 | tf_op jit(solution)/shard_map/all_to_all | solution.py:134
  17.4 0.7 and_select_fusion
  18.0 0.6 fusion.5
  22.5 1.5 constant_dynamic-slice_fusion.3
  24.0 0.1 reshape.132
  24.1 0.1 reshape.133
  24.2 0.1 reshape.134
  24.3 0.1 reshape.135
  24.4 0.8 maximum_maximum_fusion.g_ref
  25.2 0.0 all-to-all-done
  25.2 0.6 broadcast.178
  25.8 0.7 reduce.3
  26.5 0.7 reshape.131.codes_ref
  27.2 10.7 %pack.1 = bf16[16,576,256]{2,1,0:T(8,128)(2,1)} custom-call(s32[128]{0:T(128)} %reshape.131.codes_ref, bf16[512,1024]{1,0:T(8,128)(2,1)} %k_ref.3, bf16[512,1024]{1,0:T(8,128)(2,1)} %v_ref.3, bf16[16,64,256]{2,1,0:T(8,128)(2,1)} %maximum_maximum_fusion.g_ref), custom_call_target="tpu_custom_call" | custom-call | bytes 9437184 | tf_op jit(solution)/shard_map/pack/pallas_call | solution.py:34
  37.9 0.0 copy-done.2
  38.0 0.0 copy-done.3
  38.0 7.0 %all-to-all-start.1 = ((bf16[16,576,256]{2,1,0:T(8,128)(2,1)}), bf16[16,576,256]{2,1,0:T(8,128)(2,1)}, u32[]{:S(2)}, u32[]{:S(2)}) async-start(bf16[16,576,256]{2,1,0:T(8,128)(2,1)} %pack.1), calls=%async_computation.1 | async-start | bytes 9437184 | tf_op jit(solution)/shard_map/all_to_all | solution.py:155
  44.9 0.0 reduce-scatter.2.cloned.1.call-start
  45.0 5.5 %collective-permute-start.1 = (bf16[2,64,1024]{2,1,0:T(8,128)(2,1)S(1)}, bf16[2,64,1024]{2,1,0:T(8,128)(2,1)S(1)}, u32[]{:S(2)}, u32[]{:S(2)}) collective-permute-start(bf16[2,64,1024]{2,1,0:T(8,128)(2,1)S(1)} %pad_maximum_fusion.1), channel_id=1, source_target_pairs={{2,0},{4,2},{6,4},{8,6},{10,8},{12,10},{14,12},{16,14},{18,16},{20... | collective-permute-start | bytes 786440 | tf_op jit(solution)/shard_map/ppermute | solution.py:140
  50.6 0.1 collective-permute-start
  50.6 0.6 dynamic_slice.22
  53.2 145.2 %all-to-all-done.1.arr_ref = bf16[16,576,256]{2,1,0:T(8,128)(2,1)} async-done(((bf16[16,576,256]{2,1,0:T(8,128)(2,1)}), bf16[16,576,256]{2,1,0:T(8,128)(2,1)}, u32[]{:S(2)}, u32[]{:S(2)}) %all-to-all-start.1) | async-done | bytes 4718624 | tf_op jit(solution)/shard_map/all_to_all | solution.py:155
  198.4 0.8 constant_dynamic-slice_fusion
  199.1 65.1 %all_gather.6 = bf16[16,64,256]{2,1,0:T(8,128)(2,1)S(1)} all-gather(bf16[1,64,256]{2,1,0:T(8,128)(2,1)S(1)} %constant_dynamic-slice_fusion), channel_id=1, replica_groups=mesh['seq'=16,'head'=2] {'seq'}, dimensions={0}, use_global_device_ids=true | all-gather | bytes 557056 | tf_op jit(solution)/shard_map/all_gather | solution.py:158
  264.3 0.9 reshape.136.kg_ref
  265.1 0.9 reshape.137.vg_ref
  266.0 0.0 collective-permute-done.1.high_ref
  266.0 0.0 copy-start
  266.0 0.0 collective-permute-done.low_ref
  266.0 0.7 copy-done
  266.7 0.0 copy-start.1
  266.7 0.7 copy-done.1
  267.4 26.8 %attend.1 = bf16[512,1024]{1,0:T(8,128)(2,1)} custom-call(s32[64]{0:T(128)} %copy-done.2, s32[64]{0:T(128)} %copy-done.3, bf16[512,1024]{1,0:T(8,128)(2,1)} %q_ref.1, bf16[512,1024]{1,0:T(8,128)(2,1)} %k_ref.3, bf16[512,1024]{1,0:T(8,128)(2,1)} %v_ref.3, bf16[2,64,1024]{2,1,0:T(8,128)(2,1)} %copy-done.1, bf16[2,64,1024]{2,1,0:T(8,128)(2,1)} %copy-done, ...), custom_call_target="tpu_custom_call" | custom-call | flops 805306368 | bytes 8912896 | tf_op jit(solution)/shard_map/attend/pallas_call | solution.py:89
  294.2 0.0 all-gather.2.cloned.1.call-done
  294.2 10.2 %convolution_convert_fusion = bf16[512,4096]{1,0:T(8,128)(2,1)} fusion(bf16[512,1024]{1,0:T(8,128)(2,1)} %attend.1, bf16[1024,4096]{1,0:T(8,128)(2,1)} %all-gather.2.cloned.1.call-done), kind=kOutput, calls=%fused_computation | convolution fusion | flops 4297064448 | bytes 13631488 | tf_op jit(solution)/shard_map/dot_general | solution.py:166
  304.4 0.0 reduce-scatter.2.cloned.1.call-update
  304.4 8.1 %reduce-scatter.2.cloned.1.call-done = bf16[256,4096]{1,0:T(8,128)(2,1)} async-done(((bf16[512,4096]{1,0:T(8,128)(2,1)}), bf16[256,4096]{1,0:T(8,128)(2,1)}) %reduce-scatter.2.cloned.1.call-update) | async-done | bytes 2097168 | tf_op jit(solution)/shard_map/reduce_scatter | solution.py:167
  (5 shorter events, 0.1 us)
Async XLA Ops:
  6.5 287.7 %all-gather.2.cloned.1.call-start = ((), (), s32[]{:S(2)}) async-start(), calls=%async_computation.3 | async-start | bytes 8912896 | tf_op jit(solution)/shard_map/all_gather | solution.py:124
  8.0 29.9 %copy-start.2 = (s32[64]{0:T(128)}, s32[64]{0:T(128)S(1)}, u32[]{:S(2)}) copy-start(s32[64]{0:T(128)S(1)} %get-tuple-element.20.own_ref) | copy-start | bytes 772
  8.2 29.7 %copy-start.3 = (s32[64]{0:T(128)}, s32[64]{0:T(128)S(1)}, u32[]{:S(2)}) copy-start(s32[64]{0:T(128)S(1)} %convert_reduce_fusion.rank_ref) | copy-start | bytes 772
  9.0 16.2 %all-to-all-start = ((s32[16,1,8]{2,1,0:T(1,128)}), s32[16,1,8]{2,1,0:T(1,128)S(1)}, u32[]{:S(2)}, u32[]{:S(2)}) async-start(s32[16,1,8]{2,1,0:T(1,128)} %bitcast.4), calls=%async_computation | async-start | bytes 16384 | tf_op jit(solution)/shard_map/all_to_all | solution.py:134
  38.0 160.4 %all-to-all-start.1 = ((bf16[16,576,256]{2,1,0:T(8,128)(2,1)}), bf16[16,576,256]{2,1,0:T(8,128)(2,1)}, u32[]{:S(2)}, u32[]{:S(2)}) async-start(bf16[16,576,256]{2,1,0:T(8,128)(2,1)} %pack.1), calls=%async_computation.1 | async-start | bytes 9437184 | tf_op jit(solution)/shard_map/all_to_all | solution.py:155
  44.9 267.6 %reduce-scatter.2.cloned.1.call-start = ((), (), s32[]{:S(2)}) async-start(), calls=%async_computation.4 | async-start | bytes 6291456 | tf_op jit(solution)/shard_map/reduce_scatter | solution.py:167
  45.0 221.0 %collective-permute-start.1 = (bf16[2,64,1024]{2,1,0:T(8,128)(2,1)S(1)}, bf16[2,64,1024]{2,1,0:T(8,128)(2,1)S(1)}, u32[]{:S(2)}, u32[]{:S(2)}) collective-permute-start(bf16[2,64,1024]{2,1,0:T(8,128)(2,1)S(1)} %pad_maximum_fusion.1), channel_id=1, source_target_pairs={{2,0},{4,2},{6,4},{8,6},{10,8},{12,10},{14,12},{16,14},{18,16},{20... | collective-permute-start | bytes 786440 | tf_op jit(solution)/shard_map/ppermute | solution.py:140
  50.6 215.5 %collective-permute-start = (bf16[2,64,1024]{2,1,0:T(8,128)(2,1)S(1)}, bf16[2,64,1024]{2,1,0:T(8,128)(2,1)S(1)}, u32[]{:S(2)}, u32[]{:S(2)}) collective-permute-start(bf16[2,64,1024]{2,1,0:T(8,128)(2,1)S(1)} %pad_maximum_fusion), channel_id=1, source_target_pairs={{0,2},{2,4},{4,6},{6,8},{8,10},{10,12},{12,14},{14,16},{16,18},{18... | collective-permute-start | bytes 786440 | tf_op jit(solution)/shard_map/ppermute | solution.py:139
  266.0 0.7 copy-start
  266.7 0.7 copy-start.1
Sparse Core Ops, SparseCore 0:
  10.1 194.1 all-gather.1
  304.5 7.8 reduce-scatter.1

commit v2 on v1

--- a/solution.py
+++ b/solution.py
@@ -15,7 +15,7 @@
     return jnp.sum(earlier.astype(jnp.int32), axis=1)
 
 
-def pack_kernel(cap, block_len, head_dim, head_count, codes_ref, k_ref, v_ref, g_ref, o_ref):
+def pack_kernel(cap, block_len, head_dim, head_count, codes_ref, k_ref, v_ref, o_ref):
     dst = pl.program_id(0)
     for s in range(cap):
         code = codes_ref[dst * cap + s]
@@ -24,12 +24,10 @@
         rows = pl.ds(s * block_len, block_len)
         o_ref[0, rows, 0:head_dim] = k_ref[pl.ds(row, block_len), pl.ds(col, head_dim)]
         o_ref[0, rows, head_dim : 2 * head_dim] = v_ref[pl.ds(row, block_len), pl.ds(col, head_dim)]
-    o_ref[0, cap * block_len :, :] = g_ref[0]
-
-
-def pack(codes, keys, values, pieces, cap, block_len, head_dim, head_count):
-    n, extra, width = pieces.shape
-    rows = cap * block_len + extra
+
+
+def pack(codes, keys, values, n, cap, block_len, head_dim, head_count):
+    rows, width = cap * block_len, 2 * head_dim
     whole = lambda d, c: (0, 0)
     return pl.pallas_call(
         functools.partial(pack_kernel, cap, block_len, head_dim, head_count),
@@ -40,7 +38,6 @@
             in_specs=[
                 pl.BlockSpec(keys.shape, whole),
                 pl.BlockSpec(values.shape, whole),
-                pl.BlockSpec((1, extra, width), lambda d, c: (d, 0, 0)),
             ],
             out_specs=pl.BlockSpec((1, rows, width), lambda d, c: (d, 0, 0)),
         ),
@@ -48,7 +45,7 @@
             flops=0, transcendentals=0, bytes_accessed=2 * n * rows * width * 2
         ),
         name="pack",
-    )(codes, keys, values, pieces)
+    )(codes, keys, values)
 
 
 def attend_kernel(
@@ -109,6 +106,189 @@
     )(owners, ranks, q, k, v, low, high, kg, vg, arrived)
 
 
+MESH = pl.DeviceIdType.MESH
+
+
+def exchange_kernel(
+    n, source_ref, w_ref, piece_ref, first_ref, last_ref, full_ref, shared_ref, low_ref, high_ref,
+    landed, chosen, line_send, line_recv, near_send, near_recv, far_send, far_recv,
+    cut_send, cut_recv, give_send, give_recv, edge_send, edge_recv, local,
+):
+    lines = n // 4
+    me = lax.axis_index("seq")
+    z, y, x = me // 4, me // 2 % 2, me % 2
+    other_y = z * 4 + (1 - y) * 2 + x
+    other_x = z * 4 + y * 2 + 1 - x
+    half = w_ref.shape[1] // 2
+
+    barrier = pltpu.get_barrier_semaphore()
+    for k in range(1, n):
+        pl.semaphore_signal(
+            barrier, inc=1, device_id={"seq": lax.rem(me + k, n)}, device_id_type=MESH
+        )
+    pl.semaphore_wait(barrier, n - 1)
+
+    def remote(src, dst, send, recv, target):
+        return pltpu.make_async_remote_copy(
+            src_ref=src, dst_ref=dst, send_sem=send, recv_sem=recv,
+            device_id={"seq": target}, device_id_type=MESH,
+        )
+
+    def origin(side, t):
+        return (z - t if side == 0 else z + t) * 4
+
+    def exists(side, t):
+        return z - t >= 0 if side == 0 else z + t < lines
+
+    def held(side, t):
+        return w_ref if t == 0 else full_ref.at[origin(side, t) + y * 2 + x]
+
+    def along(side, t):
+        target = me + 4 if side == 0 else me - 4
+        index = origin(side, t) + y * 2 + x
+        return remote(
+            held(side, t), full_ref.at[index], line_send.at[side, t], line_recv.at[side, t], target
+        )
+
+    def passes(side, t):
+        ahead = z + 1 < lines if side == 0 else z >= 1
+        return jnp.logical_and(exists(side, t), ahead)
+
+    def near(side, t, way):
+        index = origin(side, t) + y * 2 + x
+        return remote(
+            held(side, t), full_ref.at[index], near_send.at[side, t, way],
+            near_recv.at[side, t, way], other_y if way == 0 else other_x,
+        )
+
+    def far(side, t, way):
+        index = origin(side, t) + (
+            (1 - y) * 2 + x if way == 0 else y * 2 + 1 - x
+        )
+        cols = pl.ds(way * half, half)
+        return remote(
+            full_ref.at[index, :, cols], full_ref.at[index, :, cols], far_send.at[side, t, way],
+            far_recv.at[side, t, way], other_x if way == 0 else other_y,
+        )
+
+    def sides(t):
+        return (0,) if t == 0 else (0, 1)
+
+    def advance(t):
+        for side in (0, 1):
+            if t > 0:
+                @pl.when(exists(side, t))
+                def _():
+                    along(side, t - 1).wait_recv()
+            if t < lines - 1:
+                @pl.when(passes(side, t))
+                def _():
+                    along(side, t).start()
+        for side in sides(t):
+            @pl.when(exists(side, t))
+            def _():
+                near(side, t, 0).start()
+                near(side, t, 1).start()
+
+    def forward(t):
+        for side in sides(t):
+            @pl.when(exists(side, t))
+            def _():
+                for way in (0, 1):
+                    near(side, t, way).wait_recv()
+                    far(side, t, way).start()
+
+    def cut(k):
+        target = lax.rem(me + k, n)
+        return remote(
+            piece_ref.at[target], landed.at[me], cut_send.at[k], cut_recv.at[k], target
+        )
+
+    def give(k):
+        target = lax.rem(me + k, n)
+        return remote(chosen, shared_ref.at[me], give_send.at[k], give_recv.at[k], target)
+
+    low = remote(last_ref, low_ref, edge_send.at[0], edge_recv.at[0], lax.rem(me + 1, n))
+    high = remote(first_ref, high_ref, edge_send.at[1], edge_recv.at[1], lax.rem(me + n - 1, n))
+    own_cut = pltpu.make_async_copy(piece_ref.at[me], landed.at[me], local.at[0])
+    own_rows = pltpu.make_async_copy(w_ref, full_ref.at[me], local.at[1])
+    own_give = pltpu.make_async_copy(chosen, shared_ref.at[me], local.at[2])
+
+    for k in range(1, n):
+        cut(k).start()
+    own_cut.start()
+    own_rows.start()
+    advance(0)
+    low.start()
+    high.start()
+    for k in range(1, n):
+        cut(k).wait_recv()
+    own_cut.wait()
+    chosen[...] = landed[source_ref[0]]
+    for t in range(1, lines):
+        advance(t)
+        if t == 1:
+            for k in range(1, n):
+                give(k).start()
+            own_give.start()
+        forward(t - 1)
+    forward(lines - 1)
+
+    for t in range(lines):
+        for side in (0, 1):
+            if t < lines - 1:
+                @pl.when(passes(side, t))
+                def _():
+                    along(side, t).wait_send()
+        for side in sides(t):
+            @pl.when(exists(side, t))
+            def _():
+                for way in (0, 1):
+                    near(side, t, way).wait_send()
+                    far(side, t, way).wait()
+    for k in range(1, n):
+        cut(k).wait_send()
+        give(k).wait()
+    own_give.wait()
+    own_rows.wait()
+    low.wait()
+    high.wait()
+
+
+def exchange(source, weight, pieces, first, last, n):
+    lines = n // 4
+    rows, columns = weight.shape
+    dma = pltpu.SemaphoreType.DMA
+    vmem = pl.BlockSpec(memory_space=pltpu.VMEM)
+    hbm = pl.BlockSpec(memory_space=pl.ANY)
+    kind = weight.dtype
+    return pl.pallas_call(
+        functools.partial(exchange_kernel, n),
+        out_shape=(
+            jax.ShapeDtypeStruct((n, rows, columns), kind),
+            jax.ShapeDtypeStruct(pieces.shape, kind),
+            jax.ShapeDtypeStruct(first.shape, kind),
+            jax.ShapeDtypeStruct(first.shape, kind),
+        ),
+        in_specs=[pl.BlockSpec(memory_space=pltpu.SMEM), vmem, vmem, vmem, vmem],
+        out_specs=(hbm, hbm, hbm, hbm),
+        scratch_shapes=[
+            pltpu.VMEM(pieces.shape, kind),
+            pltpu.VMEM(pieces.shape[1:], kind),
+            dma((2, lines)), dma((2, lines)),
+            dma((2, lines, 2)), dma((2, lines, 2)),
+            dma((2, lines, 2)), dma((2, lines, 2)),
+            dma((n,)), dma((n,)), dma((n,)), dma((n,)),
+            dma((2,)), dma((2,)), dma((3,)),
+        ],
+        compiler_params=pltpu.CompilerParams(collective_id=0, has_side_effects=True),
+        cost_estimate=pl.CostEstimate(
+            flops=0, transcendentals=0, bytes_accessed=40 * n * rows * columns
+        ),
+        name="exchange",
+    )(source, weight, pieces, first, last)
+
+
 def body(queries, keys, values, rand_blocks, global_blocks, out_weight):
     f32 = jnp.float32
     n = lax.axis_size("seq")
@@ -121,8 +301,6 @@
     g = global_blocks.shape[0]
     wide = 2 * head_dim
 
-    group_rows = lax.all_gather(out_weight, "seq", axis=0, tiled=True)
-
     flat_blocks = rand_blocks.reshape(entries)
     owners = flat_blocks // block_count
     head_iota = jnp.arange(entries, dtype=jnp.int32) % head_count
@@ -134,11 +312,6 @@
     incoming = lax.all_to_all(outgoing, "seq", split_axis=0, concat_axis=0, tiled=True)
     wanted = incoming.reshape(n * cap)
 
-    forward = [(i, (i + 1) % n) for i in range(n)]
-    backward = [(t, s) for s, t in forward]
-    low = lax.ppermute(jnp.stack([keys[-block_len:], values[-block_len:]]), "seq", forward)
-    high = lax.ppermute(jnp.stack([keys[:block_len], values[:block_len]]), "seq", backward)
-
     holders = global_blocks // block_count
     offsets = global_blocks % block_count * block_len
     share = n // g
@@ -151,11 +324,14 @@
     pieces = jnp.concatenate(
         [jnp.concatenate([cut(keys, m), cut(values, m)], axis=1) for m in range(g)], axis=0
     )
-    packed = pack(wanted, keys, values, pieces, cap, block_len, head_dim, head_count)
+    packed = pack(wanted, keys, values, n, cap, block_len, head_dim, head_count)
     arrived = lax.all_to_all(packed, "seq", split_axis=0, concat_axis=0, tiled=True)
-    source = holders[lax.axis_index("seq") // share]
-    mine = lax.dynamic_slice(arrived, (source, cap * block_len, 0), (1, thin, wide))
-    shared = lax.all_gather(mine, "seq", axis=0, tiled=True)
+    source = holders[lax.axis_index("seq") // share].reshape(1)
+    first = jnp.stack([keys[:block_len], values[:block_len]])
+    last = jnp.stack([keys[-block_len:], values[-block_len:]])
+    weight, packed = lax.optimization_barrier((out_weight, packed))
+    group_rows, shared, low, high = exchange(source, weight, pieces, first, last, n)
+    group_rows = group_rows.reshape(n * out_weight.shape[0], out_weight.shape[1])
     kg = shared[:, : thin // 2].reshape(g * block_len, width)
     vg = shared[:, thin // 2 :].reshape(g * block_len, width)
 

time: 321 us -> 282 us (0.88)
  Pallas kernels: 37.5 us -> 206 us
  waiting for transfers between devices: 154 us -> 18.7 us
  blocking collectives: 65.1 us -> 15.4 us
  starting transfers between devices: 20.9 us -> 4.6 us
    pallas_call x0 -> x1, Pallas kernels: none -> 171 us  [exchange(): pl.pallas_call(functools.partial(exchange_kernel, n), out_shape=(jax.Shap...]
    all_to_all x1, waiting for transfers between devices: 145 us -> 0.01 us  [body(): lax.all_to_all(packed, 'seq', split_axis=0, concat_axis=0, tiled=True)]
    all_gather x1 -> x0, blocking collectives: 65.1 us -> none  [body(): shared = lax.all_gather(mine, 'seq', axis=0, tiled=True)]
    all_to_all x0 -> x1, blocking collectives: none -> 15.4 us  [body(): lax.all_to_all(outgoing, 'seq', split_axis=0, concat_axis=0, tiled=True)]
    reduce_scatter x1, waiting for transfers between devices: 8.06 us -> 18.7 us  [body(): lax.psum_scatter(partial_value.astype(jnp.bfloat16), 'head', scatter_dime...]
    all_to_all x1 -> x0, starting transfers between devices: 8.34 us -> none  [body(): lax.all_to_all(outgoing, 'seq', split_axis=0, concat_axis=0, tiled=True)]
    ppermute x2 -> x0, starting transfers between devices: 5.59 us -> none  [the longest x1 5.53 us: body(): lax.ppermute(jnp.stack([keys[:block_len], values[:block_len]]), 'seq', ba...]
  transfers between devices with their start and end apart: 6 -> 2, of which waited for: 2 -> 1; matrix products, arithmetic and copies ran while one was open for 3% -> 2% of each run, Pallas kernels for 12% -> 61%
where the time goes in v2:
time: 282 us
  Pallas kernels  206 us (73%)
  waiting for transfers between devices  18.7 us (7%)
  between operations  17.3 us (6%)
  blocking collectives  15.4 us (5%)
  matrix products  10.2 us (4%)
  local copies, waits for them, and re-layouts  6.68 us (2%)
  starting transfers between devices  4.6 us (2%)
  other arithmetic  3.27 us (1%)
    pallas_call x1, Pallas kernels, exchange(): pl.pallas_call(functools.partial(exchange_kernel, n), out_shape=(jax.Shap...  171 us
    pallas_call x1, Pallas kernels, attend(): pl.pallas_call(functools.partial(attend_kernel, blocks, block_len, head_d...  26.6 us
    reduce_scatter x1, waiting for transfers between devices, body(): lax.psum_scatter(partial_value.astype(jnp.bfloat16), 'head', scatter_dime...  18.7 us
    all_to_all x1, blocking collectives, body(): lax.all_to_all(outgoing, 'seq', split_axis=0, concat_axis=0, tiled=True)  15.4 us
    dot_general x1, matrix products, body(): partial_value = jnp.dot(attended, group_rows, preferred_element_type=f32)  10.2 us
    pallas_call x1, Pallas kernels, pack(): pl.pallas_call(functools.partial(pack_kernel, cap, block_len, head_dim, h...  8.55 us
  transfers between devices with their start and end apart: 2, of which 1 were waited for; matrix products, arithmetic and copies ran while one was open for 2% of the time, Pallas kernels for 61%

profile of v2, /device:TPU:0, one launch (start us, length us, event | category | flops | bytes accessed | tf_op | source)
XLA Modules:
  0.0 282.0 jit_solution(11242610836070595823)
XLA Ops:
  6.5 0.0 copy-start.1
  6.5 0.0 copy-start
  6.5 0.0 copy-start.4
  6.5 0.9 reshape.133
  7.5 0.0 copy-start.2
  7.5 0.2 convert_reduce_fusion.rank_ref
  7.7 0.0 copy-start.3
  7.7 0.1 select_reduce_fusion
  7.8 0.1 all_to_all.9
  7.9 15.4 %all_to_all.14 = s32[16,1,8]{2,1,0:T(1,128)S(1)} all-to-all(s32[16,1,8]{2,1,0:T(1,128)S(1)} %bitcast.14), channel_id=1, replica_groups=mesh['seq'=16,'head'=2] {'seq'}, dimensions={0} | all-to-all | bytes 1024 | tf_op jit(solution)/shard_map/all_to_all | solution.py:312
  23.3 0.5 broadcast.178
  23.8 0.7 reduce.3
  24.5 0.6 reshape.134.codes_ref
  25.1 8.5 %pack.1 = bf16[16,512,256]{2,1,0:T(8,128)(2,1)} custom-call(s32[128]{0:T(128)} %reshape.134.codes_ref, bf16[512,1024]{1,0:T(8,128)(2,1)} %k_ref.3, bf16[512,1024]{1,0:T(8,128)(2,1)} %v_ref.3), custom_call_target="tpu_custom_call" | custom-call | bytes 8388608 | tf_op jit(solution)/shard_map/pack/pallas_call | solution.py:32
  33.7 4.6 %all-to-all-start.1 = ((bf16[16,512,256]{2,1,0:T(8,128)(2,1)}), bf16[16,512,256]{2,1,0:T(8,128)(2,1)}, u32[]{:S(2)}, u32[]{:S(2)}) async-start(bf16[16,512,256]{2,1,0:T(8,128)(2,1)} %pack.1), calls=%async_computation.1 | async-start | bytes 8388608 | tf_op jit(solution)/shard_map/all_to_all | solution.py:328
  38.2 0.0 reduce-scatter.2.cloned.1.call-start
  38.3 0.0 copy-done.4
  38.3 0.6 fusion.5
  42.7 0.0 copy-done.1
  42.7 0.0 copy-done
  42.7 0.2 slice_bitcast_fusion
  42.9 0.0 copy-done.2
  42.9 0.0 copy-done.3
  42.9 0.1 reshape.138
  43.0 0.1 reshape.136
  43.1 0.1 reshape.135
  43.2 0.1 reshape.137
  43.3 0.6 dynamic_slice.15.source_ref
  43.9 0.7 pad_maximum_fusion.1.last_ref
  44.7 0.7 pad_maximum_fusion.first_ref
  45.4 0.8 maximum_maximum_fusion.piece_ref
  46.2 170.6 %exchange.1 = (bf16[16,64,4096]{2,1,0:T(8,128)(2,1)}, bf16[16,64,256]{2,1,0:T(8,128)(2,1)}, bf16[2,64,1024]{2,1,0:T(8,128)(2,1)}, bf16[2,64,1024]{2,1,0:T(8,128)(2,1)}) custom-call(s32[1]{0:T(128)} %dynamic_slice.15.source_ref, bf16[64,4096]{1,0:T(8,128)(2,1)} %w_ref, bf16[16,64,256]{2,1,0:T(8,128)(2,1)} %maximum_maximum_fusion.piece_ref, ...), custom_call_target="tpu_custom_call" | custom-call | bytes 167772160 | tf_op jit(solution)/shard_map/exchange/pallas_call | solution.py:265
  216.9 1.1 fusion.4
  217.9 0.9 reshape.140.vg_ref
  218.8 0.9 reshape.139.kg_ref
  219.7 0.0 all-to-all-done.1.arr_ref
  219.7 26.6 %attend.1 = bf16[512,1024]{1,0:T(8,128)(2,1)} custom-call(s32[64]{0:T(128)} %copy-done.2, s32[64]{0:T(128)} %copy-done.3, bf16[512,1024]{1,0:T(8,128)(2,1)} %q_ref.1, bf16[512,1024]{1,0:T(8,128)(2,1)} %k_ref.3, bf16[512,1024]{1,0:T(8,128)(2,1)} %v_ref.3, bf16[2,64,1024]{2,1,0:T(8,128)(2,1)} %get-tuple-element.11.low_ref, ...), custom_call_target="tpu_custom_call" | custom-call | flops 805306368 | bytes 8388608 | tf_op jit(solution)/shard_map/attend/pallas_call | solution.py:86
  246.3 10.2 %convolution_convert_fusion = bf16[512,4096]{1,0:T(8,128)(2,1)} fusion(bf16[512,1024]{1,0:T(8,128)(2,1)} %attend.1, bf16[1024,4096]{1,0:T(8,128)(2,1)} %bitcast.15), kind=kOutput, calls=%fused_computation | convolution fusion | flops 4297064448 | bytes 13631488 | tf_op jit(solution)/shard_map/dot_general | solution.py:342
  256.4 0.0 reduce-scatter.2.cloned.1.call-update
  256.4 18.7 %reduce-scatter.2.cloned.1.call-done = bf16[256,4096]{1,0:T(8,128)(2,1)} async-done(((bf16[512,4096]{1,0:T(8,128)(2,1)}), bf16[256,4096]{1,0:T(8,128)(2,1)}) %reduce-scatter.2.cloned.1.call-update) | async-done | bytes 2097168 | tf_op jit(solution)/shard_map/reduce_scatter | solution.py:343
  (3 shorter events, 0.0 us)
Async XLA Ops:
  6.5 36.2 %copy-start.1 = (bf16[512,1024]{1,0:T(8,128)(2,1)S(1)}, bf16[512,1024]{1,0:T(8,128)(2,1)}, u32[]{:S(2)}) copy-start(bf16[512,1024]{1,0:T(8,128)(2,1)} %v_ref.3) | copy-start | bytes 3145732
  6.5 36.2 %copy-start = (bf16[512,1024]{1,0:T(8,128)(2,1)S(1)}, bf16[512,1024]{1,0:T(8,128)(2,1)}, u32[]{:S(2)}) copy-start(bf16[512,1024]{1,0:T(8,128)(2,1)} %k_ref.3) | copy-start | bytes 3145732
  6.5 31.7 %copy-start.4 = (s32[2]{0:T(128)S(1)}, s32[2]{0:T(128)}, u32[]{:S(2)}) copy-start(s32[2]{0:T(128)} %param.10) | copy-start | bytes 28
  7.5 35.4 %copy-start.2 = (s32[64]{0:T(128)}, s32[64]{0:T(128)S(1)}, u32[]{:S(2)}) copy-start(s32[64]{0:T(128)S(1)} %get-tuple-element.30.own_ref) | copy-start | bytes 772
  7.7 35.2 %copy-start.3 = (s32[64]{0:T(128)}, s32[64]{0:T(128)S(1)}, u32[]{:S(2)}) copy-start(s32[64]{0:T(128)S(1)} %convert_reduce_fusion.rank_ref) | copy-start | bytes 772
  33.7 186.0 %all-to-all-start.1 = ((bf16[16,512,256]{2,1,0:T(8,128)(2,1)}), bf16[16,512,256]{2,1,0:T(8,128)(2,1)}, u32[]{:S(2)}, u32[]{:S(2)}) async-start(bf16[16,512,256]{2,1,0:T(8,128)(2,1)} %pack.1), calls=%async_computation.1 | async-start | bytes 8388608 | tf_op jit(solution)/shard_map/all_to_all | solution.py:328
  38.2 236.9 %reduce-scatter.2.cloned.1.call-start = ((), (), s32[]{:S(2)}) async-start(), calls=%async_computation.3 | async-start | bytes 6291456 | tf_op jit(solution)/shard_map/reduce_scatter | solution.py:343
Sparse Core Ops, SparseCore 0:
  256.6 18.5 reduce-scatter.1
